TPU v7x, 32 devices: a whole 2x2x4 slice. The times are simulated.
32 devices in a mesh: row: 4 (over x, core), col: 8 (over z, y).
Axes of the slice: x: 2, y: 2, z: 4, core: 2. Of those that a mesh axis runs over, the one named last changes fastest.
Arguments:
- front: bfloat16 [24576, 24576], P('row', 'col'), may hold values from -6 to 6
- diag_inverse: bfloat16 [256, 256], replicated, as said below
- fill_pattern: int32 [384, 384], replicated, may hold values from 0 to 1, as said below
Outputs:
- updated: bfloat16 [24576, 24576], P('row', 'col')
Inputs may be any that keep to these rules, and one draw needn't show every extreme that they name: `fill_pattern`: symmetric, with ones on the diagonal. `diag_inverse`: lower triangular.
All inputs are finite; a program needn't handle non-finite values.
Results may differ from a plain program's by a relative error of at most 0.0045.
Values may be sent and summed in bfloat16 or wider, within the bound.
A program may use at most 128 MiB of HBM per device.

v0:
```python
import functools

import jax
import jax.numpy as jnp
from jax import lax
from jax.experimental import pallas as pl
from jax.experimental.pallas import tpu as pltpu
from jax.sharding import PartitionSpec as P

B = 64
P_SIZE = 256
LANES = 128
AHEAD = 1
MESH = pl.DeviceIdType.MESH
NT = (((1,), (1,)), ((), ()))


def nt_dot(a, b):
    return lax.dot_general(a, b, NT, preferred_element_type=jnp.float32)


def nn_dot(a, b):
    return jnp.dot(a, b, preferred_element_type=jnp.float32)


def one_hot(shape, test):
    i = lax.broadcasted_iota(jnp.int32, shape, 0)
    j = lax.broadcasted_iota(jnp.int32, shape, 1)
    return jnp.where(test(i, j), 1.0, 0.0).astype(jnp.bfloat16)


def gather_kernel(
    n_row, n_col,
    front, diag, fill, out,
    source, pan, colp, fac, colf, keep, w_lo, w_hi,
    load_sem, source_sem, row_recv, row_send, col_recv, col_send,
):
    r = lax.axis_index("row")
    c = lax.axis_index("col")
    rows, cols = out.shape
    heads = P_SIZE // B
    ratio = n_col // n_row
    half = 2 * ratio * B
    step_rows = 2 * half
    step_cols = step_rows // ratio
    chunks = rows // step_rows
    outer, inner = 4, n_col // 4
    a = c // inner
    b = c % inner
    owner = c < heads
    x, core = r // 2, r % 2
    source_row = c % n_row
    source_x, source_core = source_row // 2, source_row % 2
    parity = c // n_row
    n_x = n_row // 2

    def load(k):
        part = pl.ds(pl.multiple_of(k * step_rows, step_rows), step_rows)
        return pltpu.make_async_copy(front.at[part], out.at[part], load_sem.at[k])

    def fetch():
        return pltpu.make_async_copy(front.at[:, 0:LANES], source, source_sem)

    def row_copy(k, h, slot, target):
        return pltpu.make_async_remote_copy(
            src_ref=pan.at[k, h], dst_ref=pan.at[k, h],
            send_sem=row_send.at[k, h, slot], recv_sem=row_recv.at[k, h],
            device_id=(r, target), device_id_type=MESH,
        )

    def row_sends(k, h, act):
        a_h, b_h = h // inner, h % inner

        @pl.when(b == b_h)
        def _():
            @pl.when(jnp.logical_and(a >= a_h, a < outer - 1))
            def _():
                act(row_copy(k, h, 0, c + inner))

            @pl.when(jnp.logical_and(a <= a_h, a > 0))
            def _():
                act(row_copy(k, h, 1, c - inner))

            for d in range(1, inner):
                act(row_copy(k, h, 1 + d, a * inner + (b + d) % inner))

    def col_copy(k, src, slot, target):
        return pltpu.make_async_remote_copy(
            src_ref=src, dst_ref=colp.at[k],
            send_sem=col_send.at[k, slot], recv_sem=col_recv.at[k],
            device_id=(target, c), device_id_type=MESH,
        )

    def col_local(k):
        return pltpu.make_async_copy(pan.at[k, :, :, parity], colp.at[k], col_recv.at[k])

    is_source = r == source_row
    is_relay = jnp.logical_and(core == source_core, x != source_x)

    def col_source_sends(k, act):
        @pl.when(is_source)
        def _():
            src = pan.at[k, :, :, parity]
            for d in range(1, n_x):
                act(col_copy(k, src, d, ((x + d) % n_x) * 2 + core))
            act(col_copy(k, src, 0, x * 2 + 1 - core))

    def col_relay_sends(k, act):
        @pl.when(is_relay)
        def _():
            act(col_copy(k, colp.at[k], 0, x * 2 + 1 - core))

    @pl.when(owner)
    def _():
        fetch().start()

    for k in range(chunks):
        load(k).start()

    barrier = pltpu.get_barrier_semaphore()

    @pl.when(a > 0)
    def _():
        pl.semaphore_signal(barrier, inc=1, device_id=(r, c - inner), device_id_type=MESH)

    @pl.when(a < outer - 1)
    def _():
        pl.semaphore_signal(barrier, inc=1, device_id=(r, c + inner), device_id_type=MESH)

    for d in range(1, inner):
        pl.semaphore_signal(
            barrier, inc=1, device_id=(r, a * inner + (b + d) % inner), device_id_type=MESH
        )
    for d in range(1, n_row):
        pl.semaphore_signal(barrier, inc=1, device_id=((r + d) % n_row, c), device_id_type=MESH)

    @pl.when(owner)
    def _():
        fetch().wait()
        to_lo = one_hot((LANES, LANES), lambda i, j: (i == j) & (i < B))
        to_hi = one_hot((LANES, LANES), lambda i, j: (i + B == j) & (i < B))

        def pack(k, _):
            at = pl.multiple_of(k * step_rows, step_rows)
            both = nn_dot(source[pl.ds(at, half), :], to_lo)
            both += nn_dot(source[pl.ds(at + half, half), :], to_hi)
            pan[k, c] = both.astype(jnp.bfloat16).reshape(2, ratio, B, LANES)
            return 0

        lax.fori_loop(0, chunks, pack, 0)

    extra = jnp.where(a > 0, 1, 0) + jnp.where(a < outer - 1, 1, 0)
    pl.semaphore_wait(barrier, inner - 1 + n_row - 1 + extra)

    def own_sends(k, act):
        for h in range(heads):
            @pl.when(c == h)
            def _():
                row_sends(k, h, act)

    for k in range(min(AHEAD, chunks)):
        own_sends(k, lambda copy: copy.start())

    def spread(shift):
        return one_hot(
            (P_SIZE, heads * LANES),
            lambda i, j: (i == (j // LANES) * B + j % LANES - shift)
            & (j % LANES >= shift) & (j % LANES < shift + B),
        )

    w_lo[...] = nn_dot(diag[...], spread(0)).astype(jnp.bfloat16)
    w_hi[...] = nn_dot(diag[...], spread(B)).astype(jnp.bfloat16)

    count = fill.shape[0]
    local_rows = rows // B
    pick = one_hot((local_rows, count), lambda i, j: j == i * n_row + r)
    picked = nn_dot(pick, fill[...].astype(jnp.float32).astype(jnp.bfloat16)).astype(jnp.bfloat16)

    def make_keep(j, _):
        at = pl.multiple_of(j * step_cols, step_cols)
        widen = one_hot(
            (count, step_cols), lambda i, l: i == ((at + l) // B) * n_col + c
        )
        wide = nn_dot(picked, widen)
        i = lax.broadcasted_iota(jnp.int32, wide.shape, 0)
        l = lax.broadcasted_iota(jnp.int32, wide.shape, 1)
        live = (i * n_row + r >= heads) & (((at + l) // B) * n_col + c >= heads)
        keep[:, pl.ds(at, step_cols)] = jnp.where(live, wide, 0.0)
        return 0

    lax.fori_loop(0, cols // step_cols, make_keep, 0)

    step_blocks = step_rows // B
    to_front = one_hot((P_SIZE, LANES), lambda i, l: (i == c * B + l) & (l < B))

    def tile(i, j):
        row_at = pl.multiple_of(i * step_rows, step_rows)
        col_at = pl.multiple_of(j * step_cols, step_cols)
        part = (pl.ds(row_at, step_rows), pl.ds(col_at, step_cols))
        product = nt_dot(fac[part[0], :], colf[part[1], :])
        marks = keep[pl.ds(pl.multiple_of(i * step_blocks, step_blocks), step_blocks), part[1]]
        masked = product.reshape(step_blocks, B, step_cols) * marks[:, None, :]
        value = out[part].astype(jnp.float32) - masked.reshape(step_rows, step_cols)
        out[part] = value.astype(jnp.bfloat16)

    def arrive(k):
        @pl.when(k + AHEAD < chunks)
        def _():
            own_sends(k + AHEAD, lambda copy: copy.start())

        for h in range(heads):
            @pl.when(c != h)
            def _():
                row_copy(k, h, 0, c).wait_recv()
                row_sends(k, h, lambda copy: copy.start())

        col_source_sends(k, lambda copy: copy.start())

        @pl.when(is_source)
        def _():
            col_local(k).start()

    def factors(k):
        packed = jnp.concatenate(
            [pan[k, h].reshape(half, LANES) for h in range(heads)], axis=1
        )
        at = pl.multiple_of(k * step_rows, step_rows)
        fac[pl.ds(at, half), :] = nt_dot(packed, w_lo[...]).astype(jnp.bfloat16)
        fac[pl.ds(at + half, half), :] = nt_dot(packed, w_hi[...]).astype(jnp.bfloat16)

    def col_factors(k):
        @pl.when(is_source)
        def _():
            col_local(k).wait()

        @pl.when(jnp.logical_not(is_source))
        def _():
            col_copy(k, colp.at[k], 0, r).wait_recv()

        col_relay_sends(k, lambda copy: copy.start())
        packed = jnp.concatenate(
            [colp[k, h].reshape(2 * B, LANES) for h in range(heads)], axis=1
        )
        at = pl.multiple_of(k * step_cols, step_cols)
        colf[pl.ds(at, 2 * B), :] = nt_dot(packed, w_lo[...]).astype(jnp.bfloat16)
        colf[pl.ds(at + 2 * B, 2 * B), :] = nt_dot(packed, w_hi[...]).astype(jnp.bfloat16)

    def wave(k):
        lax.fori_loop(0, k + 1, lambda j, _: (tile(k, j), 0)[1], 0)
        lax.fori_loop(0, k, lambda i, _: (tile(i, k), 0)[1], 0)

        @pl.when(owner)
        def _():
            at = pl.ds(pl.multiple_of(k * step_rows, step_rows), step_rows)
            piece = nn_dot(fac[at, :], to_front)
            old = out[at, 0:LANES].astype(jnp.float32)
            lane = lax.broadcasted_iota(jnp.int32, old.shape, 1)
            out[at, 0:LANES] = jnp.where(lane < B, piece, old).astype(jnp.bfloat16)

    def step(k, _):
        @pl.when(k < chunks)
        def _():
            arrive(k)
            factors(k)

        @pl.when(k > 0)
        def _():
            col_factors(k - 1)
            load(k - 1).wait()
            wave(k - 1)

        return 0

    lax.fori_loop(0, chunks + 1, step, 0)

    def drain(k, _):
        for h in range(heads):
            row_sends(k, h, lambda copy: copy.wait_send())
        col_source_sends(k, lambda copy: copy.wait_send())
        col_relay_sends(k, lambda copy: copy.wait_send())
        return 0

    lax.fori_loop(0, chunks, drain, 0)


def store_kernel(value, out, sems):
    parts = sems.shape[0]
    size = value.shape[0] // parts
    copies = [
        pltpu.make_async_copy(
            value.at[pl.ds(i * size, size)], out.at[pl.ds(i * size, size)], sems.at[i]
        )
        for i in range(parts)
    ]
    for copy in copies:
        copy.start()
    for copy in copies:
        copy.wait()


def body(front, diag_inverse, fill_pattern):
    rows, cols = front.shape
    n_row = lax.axis_size("row")
    n_col = lax.axis_size("col")
    heads = P_SIZE // B
    ratio = n_col // n_row
    step_rows = 4 * ratio * B
    chunks = rows // step_rows
    inner = n_col // 4
    bf16 = jnp.bfloat16
    any_space = pl.BlockSpec(memory_space=pl.ANY)
    vmem = pl.BlockSpec(memory_space=pltpu.VMEM)
    held = pl.pallas_call(
        functools.partial(gather_kernel, n_row, n_col),
        out_shape=pltpu.VMEM((rows, cols), bf16),
        in_specs=[any_space, vmem, vmem],
        out_specs=vmem,
        scratch_shapes=[
            pltpu.VMEM((rows, LANES), bf16),
            pltpu.VMEM((chunks, heads, 2, ratio, B, LANES), bf16),
            pltpu.VMEM((chunks, heads, 2, B, LANES), bf16),
            pltpu.VMEM((rows, P_SIZE), bf16),
            pltpu.VMEM((cols, P_SIZE), bf16),
            pltpu.VMEM((rows // B, cols), jnp.float32),
            pltpu.VMEM((P_SIZE, heads * LANES), bf16),
            pltpu.VMEM((P_SIZE, heads * LANES), bf16),
            pltpu.SemaphoreType.DMA((chunks,)),
            pltpu.SemaphoreType.DMA,
            pltpu.SemaphoreType.DMA((chunks, heads)),
            pltpu.SemaphoreType.DMA((chunks, heads, inner + 1)),
            pltpu.SemaphoreType.DMA((chunks,)),
            pltpu.SemaphoreType.DMA((chunks, n_row // 2)),
        ],
        compiler_params=pltpu.CompilerParams(
            collective_id=0, has_side_effects=True, vmem_limit_bytes=20 * 2**20
        ),
        name="gather_update",
    )(front, diag_inverse, fill_pattern)
    return pl.pallas_call(
        store_kernel,
        out_shape=jax.ShapeDtypeStruct((rows, cols), bf16),
        in_specs=[any_space],
        out_specs=any_space,
        scratch_shapes=[pltpu.SemaphoreType.DMA((chunks,))],
        compiler_params=pltpu.CompilerParams(vmem_limit_bytes=20 * 2**20),
        name="store",
    )(pltpu.with_memory_space_constraint(held, pltpu.VMEM))


def solution(mesh):
    return jax.shard_map(
        body,
        mesh=mesh,
        in_specs=(P("row", "col"), P(), P()),
        out_specs=P("row", "col"),
        check_vma=False,
    )
```

profile of v0, /device:TPU:25, one launch (start us, length us, event | category | flops | bytes accessed | tf_op | source)
XLA Modules:
  0.0 252.4 jit_solution(15255157444472771241)
XLA Ops:
  0.0 240.0 %gather_update.1.value = bf16[6144,3072]{1,0:T(8,128)(2,1)S(1)} custom-call(bf16[6144,3072]{1,0:T(8,128)(2,1)} %front.1, bf16[256,256]{1,0:T(8,128)(2,1)} %diag.1, s32[384,384]{1,0:T(8,128)} %fill.1), custom_call_target="tpu_custom_call" | custom-call | tf_op jit(solution)/shard_map/gather_update/pallas_call | solution.py:313
  240.0 12.4 %store.1 = bf16[6144,3072]{1,0:T(8,128)(2,1)} custom-call(bf16[6144,3072]{1,0:T(8,128)(2,1)S(1)} %gather_update.1.value), custom_call_target="tpu_custom_call" | custom-call | tf_op jit(solution)/shard_map/store/pallas_call | solution.py:339
where the time goes:
time: 253 us; the launch traced here: 252 us
  Pallas kernels  252 us (100%)
    pallas_call x1, Pallas kernels, body(): pl.pallas_call(functools.partial(gather_kernel, n_row, n_col), out_shape=...  240 us
    pallas_call x1, Pallas kernels, body(): pl.pallas_call(store_kernel, out_shape=jax.ShapeDtypeStruct((rows, cols),...  12.4 us

commit v1 on v0

v1 whole, which is shorter than its diff:
```python
import functools

import jax
import jax.numpy as jnp
from jax import lax
from jax.experimental import pallas as pl
from jax.experimental.pallas import tpu as pltpu
from jax.sharding import PartitionSpec as P

B = 64
P_SIZE = 256
LANES = 128
SUPERS = 3
AHEAD = 4
CHAIN = 1
SLOTS = 4
MESH = pl.DeviceIdType.MESH
NT = (((1,), (1,)), ((), ()))


def nt_dot(a, b):
    return lax.dot_general(a, b, NT, preferred_element_type=jnp.float32)


def nn_dot(a, b):
    return jnp.dot(a, b, preferred_element_type=jnp.float32)


def one_hot(shape, test):
    i = lax.broadcasted_iota(jnp.int32, shape, 0)
    j = lax.broadcasted_iota(jnp.int32, shape, 1)
    return jnp.where(test(i, j), 1.0, 0.0).astype(jnp.bfloat16)


def aligned(i, size):
    return pl.ds(pl.multiple_of(i * size, size), size)


def new_tile(held, fac, colf, keep, rows_at, cols_at, step_rows, wide):
    step_blocks = step_rows // B
    product = nn_dot(fac[rows_at, :], colf[:, cols_at])
    marks = keep
    masked = product.reshape(step_blocks, B, wide) * marks[:, None, :]
    value = held[rows_at, cols_at].astype(jnp.float32) - masked.reshape(step_rows, wide)
    return value.astype(jnp.bfloat16)


def head_lanes(fac_rows, old, c):
    to_front = one_hot((P_SIZE, LANES), lambda i, l: (i == c * B + l) & (l < B))
    piece = nn_dot(fac_rows, to_front)
    lane = lax.broadcasted_iota(jnp.int32, old.shape, 1)
    return jnp.where(lane < B, piece, old.astype(jnp.float32)).astype(jnp.bfloat16)


def gather_kernel(
    n_row, n_col,
    front, diag, fill, out, fac, colf, keep,
    source, pan, colp, w_lo, w_hi, picked,
    load_sem, source_sem, row_recv, row_send, col_recv, col_send,
):
    r = lax.axis_index("row")
    c = lax.axis_index("col")
    rows, cols = out.shape
    heads = P_SIZE // B
    ratio = n_col // n_row
    sub_rows = 2 * ratio * B
    step_rows = 2 * sub_rows
    step_cols = step_rows // ratio
    half = sub_rows
    chunks = rows // step_rows
    subs = 2 * chunks
    group = chunks // SUPERS
    wide = cols // SUPERS
    outer, inner = 4, n_col // 4
    a = c // inner
    b = c % inner
    owner = c < heads
    x, core = r // 2, r % 2
    source_row = c % n_row
    source_x, source_core = source_row // 2, source_row % 2
    parity = c // n_row
    n_x = n_row // 2
    is_source = r == source_row
    is_relay = jnp.logical_and(core == source_core, x != source_x)

    def load(k):
        part = aligned(k, step_rows)
        return pltpu.make_async_copy(front.at[part], out.at[part], load_sem.at[k])

    first = min(2, chunks)

    def fetch(part):
        size = (first, chunks - first)[part] * step_rows
        at = pl.ds(part * first * step_rows, size)
        return pltpu.make_async_copy(
            front.at[at, 0:LANES], source.at[at], source_sem.at[part]
        )

    def row_copy(h, ref, recv, slot, target):
        return pltpu.make_async_remote_copy(
            src_ref=ref, dst_ref=ref,
            send_sem=row_send.at[h, slot], recv_sem=recv,
            device_id=(r, target), device_id_type=MESH,
        )

    def row_sends(h, ref, recv, act):
        a_h, b_h = h // inner, h % inner

        @pl.when(b == b_h)
        def _():
            @pl.when(jnp.logical_and(a >= a_h, a < outer - 1))
            def _():
                act(row_copy(h, ref, recv, 0, c + inner))

            @pl.when(jnp.logical_and(a <= a_h, a > 0))
            def _():
                act(row_copy(h, ref, recv, 1, c - inner))

            for d in range(1, inner):
                act(row_copy(h, ref, recv, 1 + d, a * inner + (b + d) % inner))

    def start(copy):
        copy.start()

    def own(s):
        for h in range(heads):
            @pl.when(c == h)
            def _():
                row_sends(h, pan.at[h, s], row_recv.at[h, s], start)

    def chain(s):
        for h in range(heads):
            @pl.when(jnp.logical_and(c != h, b == h % inner))
            def _():
                row_copy(h, pan.at[h, s], row_recv.at[h, s], 0, c).wait_recv()
                row_sends(h, pan.at[h, s], row_recv.at[h, s], start)

    def across(s):
        for h in range(heads):
            @pl.when(b != h % inner)
            def _():
                row_copy(h, pan.at[h, s], row_recv.at[h, s], 0, c).wait_recv()

    def col_copy(src, dst, recv, slot, target):
        return pltpu.make_async_remote_copy(
            src_ref=src, dst_ref=dst,
            send_sem=col_send.at[slot], recv_sem=recv,
            device_id=(target, c), device_id_type=MESH,
        )

    def col_local(s):
        return pltpu.make_async_copy(pan.at[:, s, parity], colp.at[s], col_recv.at[s])

    def col_source(s):
        @pl.when(is_source)
        def _():
            src = pan.at[:, s, parity]
            for d in range(1, n_x):
                target = ((x + d) % n_x) * 2 + core
                col_copy(src, colp.at[s], col_recv.at[s], d, target).start()
            col_copy(src, colp.at[s], col_recv.at[s], 0, x * 2 + 1 - core).start()
            col_local(s).start()

    def col_relay(s):
        @pl.when(is_relay)
        def _():
            copy = col_copy(colp.at[s], colp.at[s], col_recv.at[s], 0, x * 2 + 1 - core)
            copy.wait_recv()
            copy.start()

    def col_wait(s):
        @pl.when(is_source)
        def _():
            col_local(s).wait()

        @pl.when(jnp.logical_not(jnp.logical_or(is_source, is_relay)))
        def _():
            col_copy(colp.at[s], colp.at[s], col_recv.at[s], 0, r).wait_recv()

    @pl.when(owner)
    def _():
        fetch(0).start()
        fetch(1).start()

    for k in range(chunks):
        load(k).start()

    barrier = pltpu.get_barrier_semaphore()

    @pl.when(a > 0)
    def _():
        pl.semaphore_signal(barrier, inc=1, device_id=(r, c - inner), device_id_type=MESH)

    @pl.when(a < outer - 1)
    def _():
        pl.semaphore_signal(barrier, inc=1, device_id=(r, c + inner), device_id_type=MESH)

    for d in range(1, inner):
        pl.semaphore_signal(
            barrier, inc=1, device_id=(r, a * inner + (b + d) % inner), device_id_type=MESH
        )
    for d in range(1, n_row):
        pl.semaphore_signal(barrier, inc=1, device_id=((r + d) % n_row, c), device_id_type=MESH)

    to_lo = one_hot((LANES, LANES), lambda i, j: (i == j) & (i < B))
    to_hi = one_hot((LANES, LANES), lambda i, j: (i + B == j) & (i < B))

    def pack(k, _):
        at = pl.multiple_of(k * step_rows, step_rows)
        both = nn_dot(source[pl.ds(at, half), :], to_lo)
        both += nn_dot(source[pl.ds(at + half, half), :], to_hi)
        both = both.astype(jnp.bfloat16).reshape(2, ratio, B, LANES)
        pan[c, 2 * k] = both[0]
        pan[c, 2 * k + 1] = both[1]
        return 0

    @pl.when(owner)
    def _():
        fetch(0).wait()
        lax.fori_loop(0, first, pack, 0)

    extra = jnp.where(a > 0, 1, 0) + jnp.where(a < outer - 1, 1, 0)
    pl.semaphore_wait(barrier, inner - 1 + n_row - 1 + extra)

    ahead = min(AHEAD, 2 * first)
    for s in range(ahead):
        own(s)

    @pl.when(owner)
    def _():
        fetch(1).wait()
        lax.fori_loop(first, chunks, pack, 0)

    for s in range(CHAIN):
        chain(s)

    def spread(shift):
        return one_hot(
            (P_SIZE, heads * LANES),
            lambda i, j: (i == (j // LANES) * B + j % LANES - shift)
            & (j % LANES >= shift) & (j % LANES < shift + B),
        )

    w_lo[...] = nn_dot(diag[...], spread(0)).astype(jnp.bfloat16)
    w_hi[...] = nn_dot(diag[...], spread(B)).astype(jnp.bfloat16)

    count = fill.shape[0]
    local_rows = rows // B
    pick = one_hot((local_rows, count), lambda i, j: j == i * n_row + r)
    picked[...] = nn_dot(pick, fill[...].astype(jnp.float32).astype(jnp.bfloat16)).astype(
        jnp.bfloat16
    )

    step_blocks = step_rows // B

    def event(s):
        @pl.when(s + ahead < subs)
        def _():
            own(s + ahead)

        @pl.when(s + CHAIN < subs)
        def _():
            chain(s + CHAIN)

        across(s)
        col_source(s)

        @pl.when(s >= 2)
        def _():
            col_relay(s - 2)

    def row_factors(k):
        packed = jnp.concatenate(
            [pan[h, pl.ds(2 * k, 2)].reshape(half, LANES) for h in range(heads)], axis=1
        )
        at = pl.multiple_of(k * step_rows, step_rows)
        fac[pl.ds(at, half), :] = nt_dot(packed, w_lo[...]).astype(jnp.bfloat16)
        fac[pl.ds(at + half, half), :] = nt_dot(packed, w_hi[...]).astype(jnp.bfloat16)

    def col_factors(k):
        col_wait(2 * k)
        col_wait(2 * k + 1)
        packed = jnp.concatenate(
            [colp[pl.ds(2 * k, 2), h].reshape(2 * B, LANES) for h in range(heads)], axis=1
        )
        at = pl.multiple_of(k * step_cols, step_cols)
        colf[:, pl.ds(at, 2 * B)] = nt_dot(w_lo[...], packed).astype(jnp.bfloat16)
        colf[:, pl.ds(at + 2 * B, 2 * B)] = nt_dot(w_hi[...], packed).astype(jnp.bfloat16)

    def make_keep(j):
        at = pl.multiple_of(j * step_cols, step_cols)
        widen = one_hot(
            (count, step_cols), lambda i, l: i == ((at + l) // B) * n_col + c
        )
        marks = nn_dot(picked[...], widen)
        i = lax.broadcasted_iota(jnp.int32, marks.shape, 0)
        l = lax.broadcasted_iota(jnp.int32, marks.shape, 1)
        live = (i * n_row + r >= heads) & (((at + l) // B) * n_col + c >= heads)
        keep[:, pl.ds(at, step_cols)] = jnp.where(live, marks, 0.0)

    def tile(i, j):
        rows_at, cols_at = aligned(i, step_rows), aligned(j, wide)
        marks = keep[aligned(i, step_blocks), cols_at]
        out[rows_at, cols_at] = new_tile(
            out, fac, colf, marks, rows_at, cols_at, step_rows, wide
        )

        @pl.when(jnp.logical_and(owner, j == 0))
        def _():
            out[rows_at, 0:LANES] = head_lanes(fac[rows_at, :], out[rows_at, 0:LANES], c)

    def tiles(k):
        q = k // group
        t = k % group

        def one(m, _):
            fresh = m < q
            i = jnp.where(fresh, k, t * q + m - q)
            j = jnp.where(fresh, m, q - 1)
            tile(i, j)
            return 0

        lax.fori_loop(0, 2 * q, one, 0)

    def step(k, _):
        event(2 * k)

        @pl.when(k > 0)
        def _():
            row_factors(k - 1)

        make_keep(k)
        event(2 * k + 1)

        @pl.when(k > 0)
        def _():
            col_factors(k - 1)
            load(k - 1).wait()
            tiles(k - 1)

        return 0

    lax.fori_loop(0, chunks, step, 0)
    col_relay(subs - 2)
    col_relay(subs - 1)
    row_factors(chunks - 1)
    col_factors(chunks - 1)
    load(chunks - 1).wait()

    for h in range(heads):
        row_sends(h, pan.at[h], row_recv.at[h, 0], lambda copy: copy.wait_send())

    @pl.when(is_source)
    def _():
        for d in range(n_x):
            col_copy(colp, colp, col_recv.at[0], d, r).wait_send()

    @pl.when(is_relay)
    def _():
        col_copy(colp, colp, col_recv.at[0], 0, r).wait_send()


def store_kernel(n_row, n_col, held, fac, colf, keep, out, late, last, late_sem, last_sem, sem):
    c = lax.axis_index("col")
    rows, cols = out.shape
    heads = P_SIZE // B
    ratio = n_col // n_row
    step_rows = 4 * ratio * B
    chunks = rows // step_rows
    group = chunks // SUPERS
    wide = cols // SUPERS
    step_blocks = step_rows // B
    q = SUPERS - 1
    first = (group - 1) * q

    def late_copy(i):
        part = (aligned(i, step_rows), pl.ds(q * wide, wide))
        return pltpu.make_async_copy(late.at[i % SLOTS], out.at[part], late_sem.at[i % SLOTS])

    def done_copy(i, j):
        part = (aligned(i, step_rows), pl.ds(j * wide, wide))
        return pltpu.make_async_copy(held.at[part], out.at[part], sem.at[i, j])

    def is_done(i, j):
        done = i < chunks - 1
        if j == q - 1:
            done = jnp.logical_and(done, jnp.logical_or(i < first, i >= first + q))
        return done

    def value(i, j):
        rows_at, cols_at = aligned(i, step_rows), aligned(j, wide)
        marks = keep[aligned(i, step_blocks), cols_at]
        return new_tile(held, fac, colf, marks, rows_at, cols_at, step_rows, wide)

    left = [(first + d, q - 1) for d in range(q)] + [(chunks - 1, j) for j in range(q)]

    def last_copy(m):
        i, j = left[m]
        part = (aligned(i, step_rows), pl.ds(j * wide, wide))
        return pltpu.make_async_copy(last.at[m], out.at[part], last_sem.at[m])

    def step(i, _):
        for j in range(q):
            @pl.when(is_done(i, j))
            def _():
                done_copy(i, j).start()

        @pl.when(i >= SLOTS)
        def _():
            late_copy(i - SLOTS).wait()

        late[i % SLOTS] = value(i, q)
        late_copy(i).start()
        return 0

    lax.fori_loop(0, chunks, step, 0)
    for m, (i, j) in enumerate(left):
        last[m] = value(i, j)
        if j == 0:
            @pl.when(c < heads)
            def _():
                last[m, :, 0:LANES] = head_lanes(
                    fac[aligned(i, step_rows), :], last[m, :, 0:LANES], c
                )
        last_copy(m).start()

    def drain(i, _):
        for j in range(q):
            @pl.when(is_done(i, j))
            def _():
                done_copy(i, j).wait()
        return 0

    lax.fori_loop(0, chunks, drain, 0)
    for i in range(max(chunks - SLOTS, 0), chunks):
        late_copy(i).wait()
    for m in range(len(left)):
        last_copy(m).wait()


def body(front, diag_inverse, fill_pattern):
    rows, cols = front.shape
    n_row = lax.axis_size("row")
    n_col = lax.axis_size("col")
    heads = P_SIZE // B
    ratio = n_col // n_row
    step_rows = 4 * ratio * B
    chunks = rows // step_rows
    subs = 2 * chunks
    inner = n_col // 4
    wide = cols // SUPERS
    bf16 = jnp.bfloat16
    any_space = pl.BlockSpec(memory_space=pl.ANY)
    vmem = pl.BlockSpec(memory_space=pltpu.VMEM)
    parts = pl.pallas_call(
        functools.partial(gather_kernel, n_row, n_col),
        out_shape=(
            pltpu.VMEM((rows, cols), bf16),
            pltpu.VMEM((rows, P_SIZE), bf16),
            pltpu.VMEM((P_SIZE, cols), bf16),
            pltpu.VMEM((rows // B, cols), jnp.float32),
        ),
        in_specs=[any_space, vmem, vmem],
        out_specs=(vmem,) * 4,
        scratch_shapes=[
            pltpu.VMEM((rows, LANES), bf16),
            pltpu.VMEM((heads, subs, ratio, B, LANES), bf16),
            pltpu.VMEM((subs, heads, B, LANES), bf16),
            pltpu.VMEM((P_SIZE, heads * LANES), bf16),
            pltpu.VMEM((P_SIZE, heads * LANES), bf16),
            pltpu.VMEM((rows // B, fill_pattern.shape[0]), bf16),
            pltpu.SemaphoreType.DMA((chunks,)),
            pltpu.SemaphoreType.DMA((2,)),
            pltpu.SemaphoreType.DMA((heads, subs)),
            pltpu.SemaphoreType.DMA((heads, inner + 1)),
            pltpu.SemaphoreType.DMA((subs,)),
            pltpu.SemaphoreType.DMA((n_row // 2,)),
        ],
        compiler_params=pltpu.CompilerParams(
            collective_id=0, has_side_effects=True, vmem_limit_bytes=14 * 2**20
        ),
        name="gather_update",
    )(front, diag_inverse, fill_pattern)
    held = [pltpu.with_memory_space_constraint(part, pltpu.VMEM) for part in parts]
    return pl.pallas_call(
        functools.partial(store_kernel, n_row, n_col),
        out_shape=jax.ShapeDtypeStruct((rows, cols), bf16),
        in_specs=[vmem] * 4,
        out_specs=any_space,
        scratch_shapes=[
            pltpu.VMEM((SLOTS, step_rows, wide), bf16),
            pltpu.VMEM((2 * (SUPERS - 1), step_rows, wide), bf16),
            pltpu.SemaphoreType.DMA((SLOTS,)),
            pltpu.SemaphoreType.DMA((2 * (SUPERS - 1),)),
            pltpu.SemaphoreType.DMA((chunks, SUPERS - 1)),
        ],
        compiler_params=pltpu.CompilerParams(vmem_limit_bytes=14 * 2**20),
        name="store",
    )(*held)


def solution(mesh):
    return jax.shard_map(
        body,
        mesh=mesh,
        in_specs=(P("row", "col"), P(), P()),
        out_specs=P("row", "col"),
        check_vma=False,
    )
```

time: 253 us -> 101 us (0.40)
  Pallas kernels: 252 us -> 101 us
    pallas_call x1, Pallas kernels: 240 us -> 88.1 us  [body(): pl.pallas_call(functools.partial(gather_kernel, n_row, n_col), out_shape=...]
where the time goes in v1:
time: 101 us
  Pallas kernels  101 us (100%)
    pallas_call x1, Pallas kernels, body(): pl.pallas_call(functools.partial(gather_kernel, n_row, n_col), out_shape=...  88.1 us
    pallas_call x1, Pallas kernels, body(): pl.pallas_call(functools.partial(store_kernel, n_row, n_col), out_shape=j...  12.4 us

profile of v1, /device:TPU:25, one launch (start us, length us, event | category | flops | bytes accessed | tf_op | source)
XLA Modules:
  0.0 100.6 jit_solution(7535931878247515599)
XLA Ops:
  0.0 88.1 %gather_update.1 = (bf16[6144,3072]{1,0:T(8,128)(2,1)S(1)}, bf16[6144,256]{1,0:T(8,128)(2,1)S(1)}, bf16[256,3072]{1,0:T(8,128)(2,1)S(1)}, f32[96,3072]{1,0:T(8,128)S(1)}) custom-call(bf16[6144,3072]{1,0:T(8,128)(2,1)} %front.1, bf16[256,256]{1,0:T(8,128)(2,1)} %diag.1, s32[384,384]{1,0:T(8,128)} %fill.1), custom_call_target="tpu_custom_call" | custom-call | tf_op jit(solution)/shard_map/gather_update/pallas_call | solution.py:455
  88.2 12.4 %store.1 = bf16[6144,3072]{1,0:T(8,128)(2,1)} custom-call(bf16[6144,3072]{1,0:T(8,128)(2,1)S(1)} %get-tuple-element.9.held, bf16[6144,256]{1,0:T(8,128)(2,1)S(1)} %get-tuple-element.10.fac, bf16[256,3072]{1,0:T(8,128)(2,1)S(1)} %get-tuple-element.11.colf, f32[96,3072]{1,0:T(8,128)S(1)} %get-tuple-element.12.keep), custom_call_target="tpu_custom_call" | custom-call | tf_op jit(solution)/shard_map/store/pallas_call | solution.py:485

commit v2 on v1

v2 whole, which is shorter than its diff:
```python
import functools

import jax
import jax.numpy as jnp
from jax import lax
from jax.experimental import pallas as pl
from jax.experimental.pallas import tpu as pltpu
from jax.sharding import PartitionSpec as P

B = 64
P_SIZE = 256
LANES = 128
SUPERS = 3
GROUP = 8
SPLIT = 2
AHEAD = 6
CHAIN = 3
LAG = 4
GLAG = 2
BURST = 4
SLOTS = 2
MESH = pl.DeviceIdType.MESH
NT = (((1,), (1,)), ((), ()))


def nt_dot(a, b):
    return lax.dot_general(a, b, NT, preferred_element_type=jnp.float32)


def nn_dot(a, b):
    return jnp.dot(a, b, preferred_element_type=jnp.float32)


def one_hot(shape, test):
    i = lax.broadcasted_iota(jnp.int32, shape, 0)
    j = lax.broadcasted_iota(jnp.int32, shape, 1)
    return jnp.where(test(i, j), 1.0, 0.0).astype(jnp.bfloat16)


def aligned(i, size):
    return pl.ds(pl.multiple_of(i * size, size), size)


class Plan:
    def __init__(self, n_row, n_col, rows, cols, c):
        self.heads = P_SIZE // B
        self.ratio = n_col // n_row
        self.group_rows = GROUP * B
        self.groups = rows // self.group_rows
        self.per = self.groups // self.ratio
        self.wide = cols // SUPERS
        self.subs = self.groups * SPLIT
        self.pieces = GROUP // 2 // SPLIT
        self.parity = c // n_row
        self.first = (self.ratio - 1 - self.parity) * self.per
        self.burst = jnp.where(self.first == 0, 1, BURST)

    def ready(self, j):
        return self.first + self.per // SUPERS * (j + 1) + GLAG

    def rows_done(self, j):
        return jnp.minimum(
            self.groups, self.burst * jnp.maximum(self.groups - self.ready(j), 0)
        )

    def place(self, g):
        return aligned(g % self.per, GROUP), self.ratio - 1 - g // self.per


def new_tile(plan, held, fac, colf, keep, g, j):
    cols_at = pl.ds(j * plan.wide, plan.wide)
    product = nn_dot(fac[aligned(g, plan.group_rows), :], colf[:, cols_at])
    marks = keep[aligned(g, GROUP), cols_at]
    masked = product.reshape(GROUP, B, plan.wide) * marks[:, None, :]
    return (held[g, :, :, cols_at].astype(jnp.float32) - masked).astype(jnp.bfloat16)


def head_lanes(fac_rows, old, c):
    to_front = one_hot((P_SIZE, LANES), lambda i, l: (i == c * B + l) & (l < B))
    piece = nn_dot(fac_rows, to_front).reshape(old.shape)
    lane = lax.broadcasted_iota(jnp.int32, old.shape, 2)
    return jnp.where(lane < B, piece, old.astype(jnp.float32)).astype(jnp.bfloat16)


def gather_kernel(
    n_row, n_col,
    front, diag, fill, out, fac, colf, keep,
    source, pan, colp, w_lo, w_hi, picked,
    load_sem, source_sem, row_recv, row_send, col_recv, col_send,
):
    r = lax.axis_index("row")
    c = lax.axis_index("col")
    rows, cols = fac.shape[0], colf.shape[1]
    plan = Plan(n_row, n_col, rows, cols, c)
    heads, ratio, groups, per, subs = plan.heads, plan.ratio, plan.groups, plan.per, plan.subs
    group_rows = plan.group_rows
    half = group_rows // 2
    outer, inner = 4, n_col // 4
    a = c // inner
    b = c % inner
    owner = c < heads
    x, core = r // 2, r % 2
    source_row = c % n_row
    source_x, source_core = source_row // 2, source_row % 2
    n_x = n_row // 2
    is_source = r == source_row
    is_relay = jnp.logical_and(core == source_core, x != source_x)
    col_subs = per * SPLIT
    col_first = plan.first * SPLIT

    def load(g):
        blocks, remainder = plan.place(g)
        return pltpu.make_async_copy(front.at[blocks, remainder], out.at[g], load_sem.at[g])

    def fetch(part):
        at = (pl.ds(0, GROUP), pl.ds(GROUP, (per - 1) * GROUP))[part]
        return pltpu.make_async_copy(
            front.at[at, :, :, 0:LANES], source.at[at], source_sem.at[part]
        )

    def row_copy(h, ref, recv, slot, target):
        return pltpu.make_async_remote_copy(
            src_ref=ref, dst_ref=ref,
            send_sem=row_send.at[h, slot], recv_sem=recv,
            device_id=(r, target), device_id_type=MESH,
        )

    def row_sends(h, ref, recv, act):
        a_h, b_h = h // inner, h % inner

        @pl.when(b == b_h)
        def _():
            @pl.when(jnp.logical_and(a >= a_h, a < outer - 1))
            def _():
                act(row_copy(h, ref, recv, 0, c + inner))

            @pl.when(jnp.logical_and(a <= a_h, a > 0))
            def _():
                act(row_copy(h, ref, recv, 1, c - inner))

            for d in range(1, inner):
                act(row_copy(h, ref, recv, 1 + d, a * inner + (b + d) % inner))

    def start(copy):
        copy.start()

    def own(s):
        for h in range(heads):
            @pl.when(c == h)
            def _():
                row_sends(h, pan.at[h, s], row_recv.at[h, s], start)

    def chain(s):
        for h in range(heads):
            @pl.when(jnp.logical_and(c != h, b == h % inner))
            def _():
                row_copy(h, pan.at[h, s], row_recv.at[h, s], 0, c).wait_recv()
                row_sends(h, pan.at[h, s], row_recv.at[h, s], start)

    def across(s):
        for h in range(heads):
            @pl.when(b != h % inner)
            def _():
                row_copy(h, pan.at[h, s], row_recv.at[h, s], 0, c).wait_recv()

    def col_copy(src, dst, recv, slot, target):
        return pltpu.make_async_remote_copy(
            src_ref=src, dst_ref=dst,
            send_sem=col_send.at[slot], recv_sem=recv,
            device_id=(target, c), device_id_type=MESH,
        )

    def col_local(s):
        return pltpu.make_async_copy(pan.at[:, col_first + s], colp.at[s], col_recv.at[s])

    def col_source(s):
        @pl.when(is_source & (s >= 0) & (s < col_subs))
        def _():
            src = pan.at[:, col_first + s]
            for d in range(1, n_x):
                target = ((x + d) % n_x) * 2 + core
                col_copy(src, colp.at[s], col_recv.at[s], d, target).start()
            col_copy(src, colp.at[s], col_recv.at[s], 0, x * 2 + 1 - core).start()
            col_local(s).start()

    def col_relay(s):
        @pl.when(is_relay & (s >= 0) & (s < col_subs))
        def _():
            copy = col_copy(colp.at[s], colp.at[s], col_recv.at[s], 0, x * 2 + 1 - core)
            copy.wait_recv()
            copy.start()

    def col_wait(s):
        @pl.when(is_source)
        def _():
            col_local(s).wait()

        @pl.when(jnp.logical_not(jnp.logical_or(is_source, is_relay)))
        def _():
            col_copy(colp.at[s], colp.at[s], col_recv.at[s], 0, r).wait_recv()

    @pl.when(owner)
    def _():
        fetch(0).start()
        fetch(1).start()

    barrier = pltpu.get_barrier_semaphore()

    @pl.when(a > 0)
    def _():
        pl.semaphore_signal(barrier, inc=1, device_id=(r, c - inner), device_id_type=MESH)

    @pl.when(a < outer - 1)
    def _():
        pl.semaphore_signal(barrier, inc=1, device_id=(r, c + inner), device_id_type=MESH)

    for d in range(1, inner):
        pl.semaphore_signal(
            barrier, inc=1, device_id=(r, a * inner + (b + d) % inner), device_id_type=MESH
        )
    for d in range(1, n_row):
        pl.semaphore_signal(barrier, inc=1, device_id=((r + d) % n_row, c), device_id_type=MESH)

    def pack(p, _):
        to_lo = one_hot((LANES, LANES), lambda i, j: (i == j) & (i < B))
        to_hi = one_hot((LANES, LANES), lambda i, j: (i + B == j) & (i < B))
        lo = source[pl.ds(p * GROUP, GROUP // 2)].reshape(ratio * half, LANES)
        hi = source[pl.ds(p * GROUP + GROUP // 2, GROUP // 2)].reshape(ratio * half, LANES)
        both = nn_dot(lo, to_lo) + nn_dot(hi, to_hi)
        both = both.astype(jnp.bfloat16).reshape(GROUP // 2, ratio, B, LANES)
        for parity in range(ratio):
            g = (ratio - 1 - parity) * per + p
            for i in range(SPLIT):
                at = i * plan.pieces
                pan[c, g * SPLIT + i] = both[at:at + plan.pieces, parity]
        return 0

    @pl.when(owner)
    def _():
        fetch(0).wait()
        pack(0, 0)

    extra = jnp.where(a > 0, 1, 0) + jnp.where(a < outer - 1, 1, 0)
    pl.semaphore_wait(barrier, inner - 1 + n_row - 1 + extra)

    for s in range(SPLIT):
        own(s)

    @pl.when(owner)
    def _():
        fetch(1).wait()
        lax.fori_loop(1, per, pack, 0)

    for s in range(SPLIT, AHEAD):
        own(s)
    for s in range(CHAIN):
        chain(s)

    def spread(shift):
        return one_hot(
            (P_SIZE, heads * LANES),
            lambda i, j: (i == (j // LANES) * B + j % LANES - shift)
            & (j % LANES >= shift) & (j % LANES < shift + B),
        )

    w_lo[...] = nn_dot(diag[...], spread(0)).astype(jnp.bfloat16)
    w_hi[...] = nn_dot(diag[...], spread(B)).astype(jnp.bfloat16)

    def row_block(i):
        g = i // GROUP
        local = ratio * (GROUP * (g % per) + i % GROUP) + ratio - 1 - g // per
        return local * n_row + r

    count = fill.shape[0]
    pick = one_hot((rows // B, count), lambda i, j: j == row_block(i))
    picked[...] = nn_dot(pick, fill[...].astype(jnp.float32).astype(jnp.bfloat16)).astype(
        jnp.bfloat16
    )

    def event(s):
        @pl.when(s + AHEAD < subs)
        def _():
            own(s + AHEAD)

        @pl.when(s + CHAIN < subs)
        def _():
            chain(s + CHAIN)

        across(s)
        col_source(s - col_first)
        col_relay(s - col_first - LAG)

    def row_factors(g):
        packed = jnp.concatenate(
            [pan[h, pl.ds(g * SPLIT, SPLIT)].reshape(half, LANES) for h in range(heads)],
            axis=1,
        )
        at = pl.multiple_of(g * group_rows, group_rows)
        fac[pl.ds(at, half), :] = nt_dot(packed, w_lo[...]).astype(jnp.bfloat16)
        fac[pl.ds(at + half, half), :] = nt_dot(packed, w_hi[...]).astype(jnp.bfloat16)

    def col_factors(g):
        for i in range(SPLIT):
            col_wait(g * SPLIT + i)
        packed = jnp.concatenate(
            [colp[pl.ds(g * SPLIT, SPLIT), h].reshape(half, LANES) for h in range(heads)],
            axis=1,
        )
        at = pl.multiple_of(g * group_rows, group_rows)
        colf[:, pl.ds(at, half)] = nt_dot(w_lo[...], packed).astype(jnp.bfloat16)
        colf[:, pl.ds(at + half, half)] = nt_dot(w_hi[...], packed).astype(jnp.bfloat16)

    def make_keep(g):
        at = pl.multiple_of(g * group_rows, group_rows)
        widen = one_hot(
            (count, group_rows), lambda i, l: i == ((at + l) // B) * n_col + c
        )
        marks = nn_dot(picked[...], widen)
        i = lax.broadcasted_iota(jnp.int32, marks.shape, 0)
        l = lax.broadcasted_iota(jnp.int32, marks.shape, 1)
        live = (row_block(i) >= heads) & (((at + l) // B) * n_col + c >= heads)
        keep[:, pl.ds(at, group_rows)] = jnp.where(live, marks, 0.0)

    def tiles(k, j):
        def one(m, _):
            g = plan.burst * (k - plan.ready(j)) + m
            out[g, :, :, pl.ds(j * plan.wide, plan.wide)] = new_tile(
                plan, out, fac, colf, keep, g, j
            )
            if j == 0:
                @pl.when(owner)
                def _():
                    out[g, :, :, 0:LANES] = head_lanes(
                        fac[aligned(g, group_rows), :], out[g, :, :, 0:LANES], c
                    )
            return 0

        lax.fori_loop(0, jnp.where(k >= plan.ready(j), plan.burst, 0), one, 0)

    def work(k, part):
        if part == 0:
            load(k).start()

            @pl.when(k > 0)
            def _():
                row_factors(k - 1)
                load(k - 1).wait()

            @pl.when(k < per)
            def _():
                make_keep(k)

            if SPLIT == 2:
                tiles(k, 0)
        elif part == SPLIT - 1:
            g = k - GLAG - plan.first

            @pl.when((g >= 0) & (g < per))
            def _():
                col_factors(g)

            tiles(k, 2)
            if SPLIT == 2:
                tiles(k, 1)
        elif part == 1:
            tiles(k, 0)
        elif part == 2:
            tiles(k, 1)

    def step(k, _):
        for i in range(SPLIT):
            event(k * SPLIT + i)
            work(k, i)
        return 0

    lax.fori_loop(0, groups, step, 0)

    for s in range(LAG):
        col_relay(subs - LAG - col_first + s)
    row_factors(groups - 1)
    for g in range(GLAG):
        @pl.when((groups - GLAG - plan.first + g < per))
        def _():
            col_factors(groups - GLAG - plan.first + g)
    load(groups - 1).wait()

    for h in range(heads):
        row_sends(h, pan.at[h], row_recv.at[h, 0], lambda copy: copy.wait_send())

    @pl.when(is_source)
    def _():
        for d in range(n_x):
            col_copy(colp, colp, col_recv.at[0], d, r).wait_send()

    @pl.when(is_relay)
    def _():
        col_copy(colp, colp, col_recv.at[0], 0, r).wait_send()


def store_kernel(n_row, n_col, held, fac, colf, keep, out, late, late_sem, sem):
    c = lax.axis_index("col")
    plan = Plan(n_row, n_col, fac.shape[0], colf.shape[1], c)
    wide = plan.wide

    def copy(g, j, done):
        cols_at = pl.ds(j * wide, wide)
        target = out.at[(*plan.place(g), slice(None), cols_at)]
        if done:
            return pltpu.make_async_copy(held.at[g, :, :, cols_at], target, sem.at[g, j])
        slot = g % SLOTS
        return pltpu.make_async_copy(late.at[j, slot], target, late_sem.at[j, slot])

    def step(g, _):
        for j in range(SUPERS):
            @pl.when(g < plan.rows_done(j))
            def _():
                copy(g, j, True).start()

        for j in range(SUPERS):
            @pl.when(g >= plan.rows_done(j))
            def _():
                slot = g % SLOTS

                @pl.when(g - SLOTS >= plan.rows_done(j))
                def _():
                    copy(g - SLOTS, j, False).wait()

                late[j, slot] = new_tile(plan, held, fac, colf, keep, g, j)
                if j == 0:
                    @pl.when(c < plan.heads)
                    def _():
                        late[j, slot, :, :, 0:LANES] = head_lanes(
                            fac[aligned(g, plan.group_rows), :],
                            late[j, slot, :, :, 0:LANES], c,
                        )
                copy(g, j, False).start()

        return 0

    lax.fori_loop(0, plan.groups, step, 0)

    def drain(g, _):
        for j in range(SUPERS):
            @pl.when(g < plan.rows_done(j))
            def _():
                copy(g, j, True).wait()

            @pl.when((g >= plan.rows_done(j)) & (g >= plan.groups - SLOTS))
            def _():
                copy(g, j, False).wait()
        return 0

    lax.fori_loop(0, plan.groups, drain, 0)


def body(front, diag_inverse, fill_pattern):
    rows, cols = front.shape
    n_row = lax.axis_size("row")
    n_col = lax.axis_size("col")
    plan = Plan(n_row, n_col, rows, cols, 0)
    heads, ratio, groups, subs = plan.heads, plan.ratio, plan.groups, plan.subs
    split = (groups * GROUP // ratio, ratio, B, cols)
    inner = n_col // 4
    bf16 = jnp.bfloat16
    any_space = pl.BlockSpec(memory_space=pl.ANY)
    vmem = pl.BlockSpec(memory_space=pltpu.VMEM)
    parts = pl.pallas_call(
        functools.partial(gather_kernel, n_row, n_col),
        out_shape=(
            pltpu.VMEM((groups, GROUP, B, cols), bf16),
            pltpu.VMEM((rows, P_SIZE), bf16),
            pltpu.VMEM((P_SIZE, cols), bf16),
            pltpu.VMEM((rows // B, cols), jnp.float32),
        ),
        in_specs=[any_space, vmem, vmem],
        out_specs=(vmem,) * 4,
        scratch_shapes=[
            pltpu.VMEM((*split[:3], LANES), bf16),
            pltpu.VMEM((heads, subs, plan.pieces, B, LANES), bf16),
            pltpu.VMEM((plan.per * SPLIT, heads, plan.pieces, B, LANES), bf16),
            pltpu.VMEM((P_SIZE, heads * LANES), bf16),
            pltpu.VMEM((P_SIZE, heads * LANES), bf16),
            pltpu.VMEM((rows // B, fill_pattern.shape[0]), bf16),
            pltpu.SemaphoreType.DMA((groups,)),
            pltpu.SemaphoreType.DMA((2,)),
            pltpu.SemaphoreType.DMA((heads, subs)),
            pltpu.SemaphoreType.DMA((heads, inner + 1)),
            pltpu.SemaphoreType.DMA((plan.per * SPLIT,)),
            pltpu.SemaphoreType.DMA((n_row // 2,)),
        ],
        compiler_params=pltpu.CompilerParams(
            collective_id=0, has_side_effects=True, vmem_limit_bytes=14 * 2**20
        ),
        name="gather_update",
    )(front.reshape(split), diag_inverse, fill_pattern)
    held = [pltpu.with_memory_space_constraint(part, pltpu.VMEM) for part in parts]
    result = pl.pallas_call(
        functools.partial(store_kernel, n_row, n_col),
        out_shape=jax.ShapeDtypeStruct(split, bf16),
        in_specs=[vmem] * 4,
        out_specs=any_space,
        scratch_shapes=[
            pltpu.VMEM((SUPERS, SLOTS, GROUP, B, plan.wide), bf16),
            pltpu.SemaphoreType.DMA((SUPERS, SLOTS)),
            pltpu.SemaphoreType.DMA((groups, SUPERS)),
        ],
        compiler_params=pltpu.CompilerParams(vmem_limit_bytes=14 * 2**20),
        name="store",
    )(*held)
    return result.reshape(rows, cols)


def solution(mesh):
    return jax.shard_map(
        body,
        mesh=mesh,
        in_specs=(P("row", "col"), P(), P()),
        out_specs=P("row", "col"),
        check_vma=False,
    )
```

time: 101 us -> 67.1 us (0.66)
  the two profiles are of different devices: /device:TPU:25 before, /device:TPU:9 now
where the time goes in v2:
time: 67.1 us; the launch traced here: 67 us
  Pallas kernels  67 us (100%)
    pallas_call x1, Pallas kernels, body(): pl.pallas_call(functools.partial(gather_kernel, n_row, n_col), out_shape=...  51.6 us
    pallas_call x1, Pallas kernels, body(): pl.pallas_call(functools.partial(store_kernel, n_row, n_col), out_shape=j...  15.3 us

profile of v2, /device:TPU:9, one launch (start us, length us, event | category | flops | bytes accessed | tf_op | source)
XLA Modules:
  0.0 67.0 jit_solution(14853013216594307490)
XLA Ops:
  0.0 51.6 %gather_update.1 = (bf16[12,8,64,3072]{3,2,1,0:T(8,128)(2,1)S(1)}, bf16[6144,256]{1,0:T(8,128)(2,1)S(1)}, bf16[256,3072]{1,0:T(8,128)(2,1)S(1)}, f32[96,3072]{1,0:T(8,128)S(1)}) custom-call(bf16[48,2,64,3072]{3,2,1,0:T(8,128)(2,1)} %bitcast.2, bf16[256,256]{1,0:T(8,128)(2,1)} %diag.1, s32[384,384]{1,0:T(8,128)} %fill.1), custom_call_target="tpu_custom_call" | custom-call | tf_op jit(solution)/shard_map/gather_update/pallas_call | solution.py:467
  51.6 15.3 %store.1 = bf16[48,2,64,3072]{3,2,1,0:T(8,128)(2,1)} custom-call(bf16[12,8,64,3072]{3,2,1,0:T(8,128)(2,1)S(1)} %get-tuple-element.9.held, bf16[6144,256]{1,0:T(8,128)(2,1)S(1)} %get-tuple-element.10.fac, bf16[256,3072]{1,0:T(8,128)(2,1)S(1)} %get-tuple-element.11.colf, f32[96,3072]{1,0:T(8,128)S(1)} %get-tuple-element.12.keep), custom_call_target="tpu_custom_call" | custom-call | tf_op jit(solution)/shard_map/store/pallas_call | solution.py:497

commit v3 on v2

--- a/solution.py
+++ b/solution.py
@@ -15,10 +15,11 @@
 SPLIT = 2
 AHEAD = 6
 CHAIN = 3
-LAG = 4
-GLAG = 2
-BURST = 4
-SLOTS = 2
+LAG = 6
+GLAG = 3
+BURST = 2
+QUIET = 0
+SLOTS = 3
 MESH = pl.DeviceIdType.MESH
 NT = (((1,), (1,)), ((), ()))
 
@@ -51,20 +52,21 @@
         self.wide = cols // SUPERS
         self.subs = self.groups * SPLIT
         self.pieces = GROUP // 2 // SPLIT
-        self.parity = c // n_row
-        self.first = (self.ratio - 1 - self.parity) * self.per
-        self.burst = jnp.where(self.first == 0, 1, BURST)
-
-    def ready(self, j):
-        return self.first + self.per // SUPERS * (j + 1) + GLAG
+        self.turn = self.ratio - 1 - c // n_row
+
+    def mine(self, g):
+        return (g >= 0) & (g % self.ratio == self.turn)
+
+    def tiles_to(self, k, j):
+        last = self.ratio * (self.per // SUPERS * (j + 1) - 1) + self.turn
+        k = jnp.minimum(k, self.groups - 1 - QUIET)
+        return jnp.clip(BURST * (k - last - GLAG), 0, jnp.maximum(k, 0))
 
     def rows_done(self, j):
-        return jnp.minimum(
-            self.groups, self.burst * jnp.maximum(self.groups - self.ready(j), 0)
-        )
+        return self.tiles_to(self.groups, j)
 
     def place(self, g):
-        return aligned(g % self.per, GROUP), self.ratio - 1 - g // self.per
+        return aligned(g // self.ratio, GROUP), self.ratio - 1 - g % self.ratio
 
 
 def new_tile(plan, held, fac, colf, keep, g, j):
@@ -73,13 +75,6 @@
     marks = keep[aligned(g, GROUP), cols_at]
     masked = product.reshape(GROUP, B, plan.wide) * marks[:, None, :]
     return (held[g, :, :, cols_at].astype(jnp.float32) - masked).astype(jnp.bfloat16)
-
-
-def head_lanes(fac_rows, old, c):
-    to_front = one_hot((P_SIZE, LANES), lambda i, l: (i == c * B + l) & (l < B))
-    piece = nn_dot(fac_rows, to_front).reshape(old.shape)
-    lane = lax.broadcasted_iota(jnp.int32, old.shape, 2)
-    return jnp.where(lane < B, piece, old.astype(jnp.float32)).astype(jnp.bfloat16)
 
 
 def gather_kernel(
@@ -105,8 +100,9 @@
     n_x = n_row // 2
     is_source = r == source_row
     is_relay = jnp.logical_and(core == source_core, x != source_x)
-    col_subs = per * SPLIT
-    col_first = plan.first * SPLIT
+
+    def col_slot(s):
+        return s // SPLIT // ratio * SPLIT + s % SPLIT
 
     def load(g):
         blocks, remainder = plan.place(g)
@@ -149,19 +145,32 @@
             @pl.when(c == h)
             def _():
                 row_sends(h, pan.at[h, s], row_recv.at[h, s], start)
-
-    def chain(s):
-        for h in range(heads):
-            @pl.when(jnp.logical_and(c != h, b == h % inner))
-            def _():
-                row_copy(h, pan.at[h, s], row_recv.at[h, s], 0, c).wait_recv()
-                row_sends(h, pan.at[h, s], row_recv.at[h, s], start)
+                col_piece(h, s)
+
+    def chain(h, s, when=True):
+        @pl.when((c != h) & (b == h % inner) & when & (s < subs))
+        def _():
+            row_copy(h, pan.at[h, s], row_recv.at[h, s], 0, c).wait_recv()
+            row_sends(h, pan.at[h, s], row_recv.at[h, s], start)
+            col_piece(h, s)
+
+    def near(h):
+        return (a > h // inner) & (h // inner == (heads - 1) // inner)
 
     def across(s):
         for h in range(heads):
             @pl.when(b != h % inner)
             def _():
                 row_copy(h, pan.at[h, s], row_recv.at[h, s], 0, c).wait_recv()
+                col_piece(h, s)
+
+    def col_piece(h, s):
+        @pl.when(is_source & plan.mine(s // SPLIT))
+        def _():
+            t = col_slot(s)
+            for d in range(1, n_x):
+                target = ((x + d) % n_x) * 2 + core
+                col_copy(pan.at[h, s], colp.at[t, h], col_recv.at[t], d, target).start()
 
     def col_copy(src, dst, recv, slot, target):
         return pltpu.make_async_remote_copy(
@@ -171,22 +180,22 @@
         )
 
     def col_local(s):
-        return pltpu.make_async_copy(pan.at[:, col_first + s], colp.at[s], col_recv.at[s])
+        t = col_slot(s)
+        return pltpu.make_async_copy(pan.at[:, s], colp.at[t], col_recv.at[t])
+
+    def col_mate(src, t):
+        return col_copy(src, colp.at[t], col_recv.at[t], 0, x * 2 + 1 - core)
 
     def col_source(s):
-        @pl.when(is_source & (s >= 0) & (s < col_subs))
-        def _():
-            src = pan.at[:, col_first + s]
-            for d in range(1, n_x):
-                target = ((x + d) % n_x) * 2 + core
-                col_copy(src, colp.at[s], col_recv.at[s], d, target).start()
-            col_copy(src, colp.at[s], col_recv.at[s], 0, x * 2 + 1 - core).start()
+        @pl.when(is_source & plan.mine(s // SPLIT))
+        def _():
+            col_mate(pan.at[:, s], col_slot(s)).start()
             col_local(s).start()
 
     def col_relay(s):
-        @pl.when(is_relay & (s >= 0) & (s < col_subs))
-        def _():
-            copy = col_copy(colp.at[s], colp.at[s], col_recv.at[s], 0, x * 2 + 1 - core)
+        @pl.when(is_relay & (s >= 0) & plan.mine(s // SPLIT))
+        def _():
+            copy = col_mate(colp.at[col_slot(s)], col_slot(s))
             copy.wait_recv()
             copy.start()
 
@@ -197,7 +206,8 @@
 
         @pl.when(jnp.logical_not(jnp.logical_or(is_source, is_relay)))
         def _():
-            col_copy(colp.at[s], colp.at[s], col_recv.at[s], 0, r).wait_recv()
+            t = col_slot(s)
+            col_copy(colp.at[t], colp.at[t], col_recv.at[t], 0, r).wait_recv()
 
     @pl.when(owner)
     def _():
@@ -229,7 +239,7 @@
         both = nn_dot(lo, to_lo) + nn_dot(hi, to_hi)
         both = both.astype(jnp.bfloat16).reshape(GROUP // 2, ratio, B, LANES)
         for parity in range(ratio):
-            g = (ratio - 1 - parity) * per + p
+            g = p * ratio + ratio - 1 - parity
             for i in range(SPLIT):
                 at = i * plan.pieces
                 pan[c, g * SPLIT + i] = both[at:at + plan.pieces, parity]
@@ -253,8 +263,12 @@
 
     for s in range(SPLIT, AHEAD):
         own(s)
-    for s in range(CHAIN):
-        chain(s)
+    for h in reversed(range(heads)):
+        for s in range(AHEAD):
+            chain(h, s, near(h))
+    for h in reversed(range(heads)):
+        for s in range(CHAIN):
+            chain(h, s, jnp.logical_not(near(h)))
 
     def spread(shift):
         return one_hot(
@@ -268,7 +282,7 @@
 
     def row_block(i):
         g = i // GROUP
-        local = ratio * (GROUP * (g % per) + i % GROUP) + ratio - 1 - g // per
+        local = ratio * (GROUP * (g // ratio) + i % GROUP) + ratio - 1 - g % ratio
         return local * n_row + r
 
     count = fill.shape[0]
@@ -282,13 +296,12 @@
         def _():
             own(s + AHEAD)
 
-        @pl.when(s + CHAIN < subs)
-        def _():
-            chain(s + CHAIN)
+        for h in reversed(range(heads)):
+            chain(h, s + jnp.where(near(h), AHEAD, CHAIN))
 
         across(s)
-        col_source(s - col_first)
-        col_relay(s - col_first - LAG)
+        col_source(s)
+        col_relay(s - LAG)
 
     def row_factors(g):
         packed = jnp.concatenate(
@@ -302,13 +315,27 @@
     def col_factors(g):
         for i in range(SPLIT):
             col_wait(g * SPLIT + i)
+        p = g // ratio
         packed = jnp.concatenate(
-            [colp[pl.ds(g * SPLIT, SPLIT), h].reshape(half, LANES) for h in range(heads)],
+            [colp[pl.ds(p * SPLIT, SPLIT), h].reshape(half, LANES) for h in range(heads)],
             axis=1,
         )
-        at = pl.multiple_of(g * group_rows, group_rows)
+        at = pl.multiple_of(p * group_rows, group_rows)
         colf[:, pl.ds(at, half)] = nt_dot(w_lo[...], packed).astype(jnp.bfloat16)
         colf[:, pl.ds(at + half, half)] = nt_dot(w_hi[...], packed).astype(jnp.bfloat16)
+
+        @pl.when(owner & (p == 0))
+        def _():
+            unit = one_hot((P_SIZE, LANES), lambda i, l: i == c * B + l)
+            lane = lax.broadcasted_iota(jnp.int32, unit.shape, 1)
+            colf[:, 0:LANES] = jnp.where(lane < B, -unit, colf[:, 0:LANES])
+
+    def clear(g):
+        @pl.when(owner)
+        def _():
+            old = out[g, :, :, 0:LANES]
+            lane = lax.broadcasted_iota(jnp.int32, old.shape, 2)
+            out[g, :, :, 0:LANES] = jnp.where(lane < B, jnp.zeros_like(old), old)
 
     def make_keep(g):
         at = pl.multiple_of(g * group_rows, group_rows)
@@ -318,24 +345,21 @@
         marks = nn_dot(picked[...], widen)
         i = lax.broadcasted_iota(jnp.int32, marks.shape, 0)
         l = lax.broadcasted_iota(jnp.int32, marks.shape, 1)
-        live = (row_block(i) >= heads) & (((at + l) // B) * n_col + c >= heads)
-        keep[:, pl.ds(at, group_rows)] = jnp.where(live, marks, 0.0)
+        marks = jnp.where(row_block(i) >= heads, marks, 0.0)
+        head = ((at + l) // B) * n_col + c < heads
+        keep[:, pl.ds(at, group_rows)] = jnp.where(head, 1.0, marks)
+
+    def tile(g, j):
+        out[g, :, :, pl.ds(j * plan.wide, plan.wide)] = new_tile(
+            plan, out, fac, colf, keep, g, j
+        )
 
     def tiles(k, j):
-        def one(m, _):
-            g = plan.burst * (k - plan.ready(j)) + m
-            out[g, :, :, pl.ds(j * plan.wide, plan.wide)] = new_tile(
-                plan, out, fac, colf, keep, g, j
-            )
-            if j == 0:
-                @pl.when(owner)
-                def _():
-                    out[g, :, :, 0:LANES] = head_lanes(
-                        fac[aligned(g, group_rows), :], out[g, :, :, 0:LANES], c
-                    )
+        def one(g, _):
+            tile(g, j)
             return 0
 
-        lax.fori_loop(0, jnp.where(k >= plan.ready(j), plan.burst, 0), one, 0)
+        lax.fori_loop(plan.tiles_to(k - 1, j), plan.tiles_to(k, j), one, 0)
 
     def work(k, part):
         if part == 0:
@@ -345,6 +369,7 @@
             def _():
                 row_factors(k - 1)
                 load(k - 1).wait()
+                clear(k - 1)
 
             @pl.when(k < per)
             def _():
@@ -353,11 +378,9 @@
             if SPLIT == 2:
                 tiles(k, 0)
         elif part == SPLIT - 1:
-            g = k - GLAG - plan.first
-
-            @pl.when((g >= 0) & (g < per))
-            def _():
-                col_factors(g)
+            @pl.when(plan.mine(k - GLAG))
+            def _():
+                col_factors(k - GLAG)
 
             tiles(k, 2)
             if SPLIT == 2:
@@ -375,14 +398,15 @@
 
     lax.fori_loop(0, groups, step, 0)
 
-    for s in range(LAG):
-        col_relay(subs - LAG - col_first + s)
     row_factors(groups - 1)
-    for g in range(GLAG):
-        @pl.when((groups - GLAG - plan.first + g < per))
-        def _():
-            col_factors(groups - GLAG - plan.first + g)
     load(groups - 1).wait()
+    clear(groups - 1)
+    for i in range(LAG):
+        col_relay(subs - LAG + i)
+    for i in range(GLAG):
+        @pl.when(plan.mine(groups - GLAG + i))
+        def _():
+            col_factors(groups - GLAG + i)
 
     for h in range(heads):
         row_sends(h, pan.at[h], row_recv.at[h, 0], lambda copy: copy.wait_send())
@@ -410,29 +434,23 @@
         slot = g % SLOTS
         return pltpu.make_async_copy(late.at[j, slot], target, late_sem.at[j, slot])
 
-    def step(g, _):
+    def step(i, _):
         for j in range(SUPERS):
-            @pl.when(g < plan.rows_done(j))
-            def _():
-                copy(g, j, True).start()
-
+            @pl.when(i < plan.rows_done(j))
+            def _():
+                copy(i, j, True).start()
+
+        g = plan.groups - 1 - i
         for j in range(SUPERS):
             @pl.when(g >= plan.rows_done(j))
             def _():
                 slot = g % SLOTS
 
-                @pl.when(g - SLOTS >= plan.rows_done(j))
+                @pl.when(i >= SLOTS)
                 def _():
-                    copy(g - SLOTS, j, False).wait()
+                    copy(g + SLOTS, j, False).wait()
 
                 late[j, slot] = new_tile(plan, held, fac, colf, keep, g, j)
-                if j == 0:
-                    @pl.when(c < plan.heads)
-                    def _():
-                        late[j, slot, :, :, 0:LANES] = head_lanes(
-                            fac[aligned(g, plan.group_rows), :],
-                            late[j, slot, :, :, 0:LANES], c,
-                        )
                 copy(g, j, False).start()
 
         return 0
@@ -445,7 +463,7 @@
             def _():
                 copy(g, j, True).wait()
 
-            @pl.when((g >= plan.rows_done(j)) & (g >= plan.groups - SLOTS))
+            @pl.when((g >= plan.rows_done(j)) & (g < plan.rows_done(j) + SLOTS))
             def _():
                 copy(g, j, False).wait()
         return 0

time: 67.1 us -> 64 us (0.954)
  the two profiles are of different devices: /device:TPU:9 before, /device:TPU:25 now
where the time goes in v3:
time: 64 us; the launch traced here: 63.8 us
  Pallas kernels  63.8 us (100%)
    pallas_call x1, Pallas kernels, body(): pl.pallas_call(functools.partial(gather_kernel, n_row, n_col), out_shape=...  51 us
    pallas_call x1, Pallas kernels, body(): pl.pallas_call(functools.partial(store_kernel, n_row, n_col), out_shape=j...  12.8 us

profile of v3, /device:TPU:25, one launch (start us, length us, event | category | flops | bytes accessed | tf_op | source)
XLA Modules:
  0.0 63.8 jit_solution(15410355613952111613)
XLA Ops:
  0.0 51.0 %gather_update.1 = (bf16[12,8,64,3072]{3,2,1,0:T(8,128)(2,1)S(1)}, bf16[6144,256]{1,0:T(8,128)(2,1)S(1)}, bf16[256,3072]{1,0:T(8,128)(2,1)S(1)}, f32[96,3072]{1,0:T(8,128)S(1)}) custom-call(bf16[48,2,64,3072]{3,2,1,0:T(8,128)(2,1)} %bitcast.2, bf16[256,256]{1,0:T(8,128)(2,1)} %diag.1, s32[384,384]{1,0:T(8,128)} %fill.1), custom_call_target="tpu_custom_call" | custom-call | tf_op jit(solution)/shard_map/gather_update/pallas_call | solution.py:485
  51.0 12.8 %store.1 = bf16[48,2,64,3072]{3,2,1,0:T(8,128)(2,1)} custom-call(bf16[12,8,64,3072]{3,2,1,0:T(8,128)(2,1)S(1)} %get-tuple-element.9.held, bf16[6144,256]{1,0:T(8,128)(2,1)S(1)} %get-tuple-element.10.fac, bf16[256,3072]{1,0:T(8,128)(2,1)S(1)} %get-tuple-element.11.colf, f32[96,3072]{1,0:T(8,128)S(1)} %get-tuple-element.12.keep), custom_call_target="tpu_custom_call" | custom-call | tf_op jit(solution)/shard_map/store/pallas_call | solution.py:515

commit v4 on v3

--- a/solution.py
+++ b/solution.py
@@ -13,12 +13,14 @@
 SUPERS = 3
 GROUP = 8
 SPLIT = 2
-AHEAD = 6
+AHEAD = 4
+CROSS = 10
 CHAIN = 3
-LAG = 6
-GLAG = 3
+LAG = 4
+GLAG = 2
 BURST = 2
-QUIET = 0
+QUIET = 1
+PRELOAD = 6
 SLOTS = 3
 MESH = pl.DeviceIdType.MESH
 NT = (((1,), (1,)), ((), ()))
@@ -54,11 +56,15 @@
         self.pieces = GROUP // 2 // SPLIT
         self.turn = self.ratio - 1 - c // n_row
 
+    def swap(self, g):
+        low, high = self.groups - 3, self.groups - 2
+        return jnp.where(g == low, high, jnp.where(g == high, low, g))
+
     def mine(self, g):
-        return (g >= 0) & (g % self.ratio == self.turn)
+        return (g >= 0) & (self.swap(g) % self.ratio == self.turn)
 
     def tiles_to(self, k, j):
-        last = self.ratio * (self.per // SUPERS * (j + 1) - 1) + self.turn
+        last = self.swap(self.ratio * (self.per // SUPERS * (j + 1) - 1) + self.turn)
         k = jnp.minimum(k, self.groups - 1 - QUIET)
         return jnp.clip(BURST * (k - last - GLAG), 0, jnp.maximum(k, 0))
 
@@ -66,7 +72,8 @@
         return self.tiles_to(self.groups, j)
 
     def place(self, g):
-        return aligned(g // self.ratio, GROUP), self.ratio - 1 - g % self.ratio
+        turn = self.swap(g)
+        return aligned(turn // self.ratio, GROUP), self.ratio - 1 - turn % self.ratio
 
 
 def new_tile(plan, held, fac, colf, keep, g, j):
@@ -102,7 +109,7 @@
     is_relay = jnp.logical_and(core == source_core, x != source_x)
 
     def col_slot(s):
-        return s // SPLIT // ratio * SPLIT + s % SPLIT
+        return plan.swap(s // SPLIT) // ratio * SPLIT + s % SPLIT
 
     def load(g):
         blocks, remainder = plan.place(g)
@@ -121,31 +128,49 @@
             device_id=(r, target), device_id_type=MESH,
         )
 
-    def row_sends(h, ref, recv, act):
+    slots = tuple(range(inner + 1))
+
+    def row_sends(h, ref, recv, act, slots=slots):
         a_h, b_h = h // inner, h % inner
 
         @pl.when(b == b_h)
         def _():
-            @pl.when(jnp.logical_and(a >= a_h, a < outer - 1))
-            def _():
-                act(row_copy(h, ref, recv, 0, c + inner))
-
-            @pl.when(jnp.logical_and(a <= a_h, a > 0))
-            def _():
-                act(row_copy(h, ref, recv, 1, c - inner))
+            if 0 in slots:
+                @pl.when(jnp.logical_and(a >= a_h, a < outer - 1))
+                def _():
+                    act(row_copy(h, ref, recv, 0, c + inner))
+
+            if 1 in slots:
+                @pl.when(jnp.logical_and(a <= a_h, a > 0))
+                def _():
+                    act(row_copy(h, ref, recv, 1, c - inner))
 
             for d in range(1, inner):
-                act(row_copy(h, ref, recv, 1 + d, a * inner + (b + d) % inner))
+                if 1 + d in slots:
+                    act(row_copy(h, ref, recv, 1 + d, a * inner + (b + d) % inner))
 
     def start(copy):
         copy.start()
 
+    def cross(h):
+        top = (heads - 1) // inner
+        if top == 0:
+            return ()
+        return (0,) if h // inner < top else (1,)
+
     def own(s):
         for h in range(heads):
-            @pl.when(c == h)
-            def _():
-                row_sends(h, pan.at[h, s], row_recv.at[h, s], start)
+            @pl.when((c == h) & (s < subs))
+            def _():
+                rest = tuple(slot for slot in slots if slot not in cross(h))
+                row_sends(h, pan.at[h, s], row_recv.at[h, s], start, rest)
                 col_piece(h, s)
+
+    def own_cross(s):
+        for h in range(heads):
+            @pl.when((c == h) & (s < subs))
+            def _():
+                row_sends(h, pan.at[h, s], row_recv.at[h, s], start, cross(h))
 
     def chain(h, s, when=True):
         @pl.when((c != h) & (b == h % inner) & when & (s < subs))
@@ -213,6 +238,9 @@
     def _():
         fetch(0).start()
         fetch(1).start()
+
+    early = jnp.where(owner, 0, min(PRELOAD, groups))
+    lax.fori_loop(0, early, lambda g, _: (load(g).start(), 0)[1], 0)
 
     barrier = pltpu.get_barrier_semaphore()
 
@@ -239,7 +267,7 @@
         both = nn_dot(lo, to_lo) + nn_dot(hi, to_hi)
         both = both.astype(jnp.bfloat16).reshape(GROUP // 2, ratio, B, LANES)
         for parity in range(ratio):
-            g = p * ratio + ratio - 1 - parity
+            g = plan.swap(p * ratio + ratio - 1 - parity)
             for i in range(SPLIT):
                 at = i * plan.pieces
                 pan[c, g * SPLIT + i] = both[at:at + plan.pieces, parity]
@@ -253,16 +281,23 @@
     extra = jnp.where(a > 0, 1, 0) + jnp.where(a < outer - 1, 1, 0)
     pl.semaphore_wait(barrier, inner - 1 + n_row - 1 + extra)
 
-    for s in range(SPLIT):
-        own(s)
+    sent = SPLIT * ratio
+    for s in range(sent):
+        if s < AHEAD:
+            own(s)
+        if s < CROSS:
+            own_cross(s)
 
     @pl.when(owner)
     def _():
         fetch(1).wait()
         lax.fori_loop(1, per, pack, 0)
 
-    for s in range(SPLIT, AHEAD):
-        own(s)
+    for s in range(sent, max(AHEAD, CROSS)):
+        if s < AHEAD:
+            own(s)
+        if s < CROSS:
+            own_cross(s)
     for h in reversed(range(heads)):
         for s in range(AHEAD):
             chain(h, s, near(h))
@@ -281,7 +316,7 @@
     w_hi[...] = nn_dot(diag[...], spread(B)).astype(jnp.bfloat16)
 
     def row_block(i):
-        g = i // GROUP
+        g = plan.swap(i // GROUP)
         local = ratio * (GROUP * (g // ratio) + i % GROUP) + ratio - 1 - g % ratio
         return local * n_row + r
 
@@ -292,10 +327,8 @@
     )
 
     def event(s):
-        @pl.when(s + AHEAD < subs)
-        def _():
-            own(s + AHEAD)
-
+        own(s + AHEAD)
+        own_cross(s + CROSS)
         for h in reversed(range(heads)):
             chain(h, s + jnp.where(near(h), AHEAD, CHAIN))
 
@@ -315,7 +348,7 @@
     def col_factors(g):
         for i in range(SPLIT):
             col_wait(g * SPLIT + i)
-        p = g // ratio
+        p = plan.swap(g) // ratio
         packed = jnp.concatenate(
             [colp[pl.ds(p * SPLIT, SPLIT), h].reshape(half, LANES) for h in range(heads)],
             axis=1,
@@ -363,7 +396,9 @@
 
     def work(k, part):
         if part == 0:
-            load(k).start()
+            @pl.when(k + early < groups)
+            def _():
+                load(k + early).start()
 
             @pl.when(k > 0)
             def _():

time: 64 us -> 61.9 us (0.967)
  Pallas kernels: 63.8 us -> 61.6 us
    pallas_call x1, Pallas kernels: 51 us -> 48.7 us  [body(): pl.pallas_call(functools.partial(gather_kernel, n_row, n_col), out_shape=...]
where the time goes in v4:
time: 61.9 us; the launch traced here: 61.6 us
  Pallas kernels  61.6 us (100%)
    pallas_call x1, Pallas kernels, body(): pl.pallas_call(functools.partial(gather_kernel, n_row, n_col), out_shape=...  48.7 us
    pallas_call x1, Pallas kernels, body(): pl.pallas_call(functools.partial(store_kernel, n_row, n_col), out_shape=j...  12.9 us

profile of v4, /device:TPU:25, one launch (start us, length us, event | category | flops | bytes accessed | tf_op | source)
XLA Modules:
  0.0 61.6 jit_solution(6358570526195335072)
XLA Ops:
  0.0 48.7 %gather_update.1 = (bf16[12,8,64,3072]{3,2,1,0:T(8,128)(2,1)S(1)}, bf16[6144,256]{1,0:T(8,128)(2,1)S(1)}, bf16[256,3072]{1,0:T(8,128)(2,1)S(1)}, f32[96,3072]{1,0:T(8,128)S(1)}) custom-call(bf16[48,2,64,3072]{3,2,1,0:T(8,128)(2,1)} %bitcast.2, bf16[256,256]{1,0:T(8,128)(2,1)} %diag.1, s32[384,384]{1,0:T(8,128)} %fill.1), custom_call_target="tpu_custom_call" | custom-call | tf_op jit(solution)/shard_map/gather_update/pallas_call | solution.py:520
  48.7 12.9 %store.1 = bf16[48,2,64,3072]{3,2,1,0:T(8,128)(2,1)} custom-call(bf16[12,8,64,3072]{3,2,1,0:T(8,128)(2,1)S(1)} %get-tuple-element.9.held, bf16[6144,256]{1,0:T(8,128)(2,1)S(1)} %get-tuple-element.10.fac, bf16[256,3072]{1,0:T(8,128)(2,1)S(1)} %get-tuple-element.11.colf, f32[96,3072]{1,0:T(8,128)S(1)} %get-tuple-element.12.keep), custom_call_target="tpu_custom_call" | custom-call | tf_op jit(solution)/shard_map/store/pallas_call | solution.py:550
